TPU v7x, 128 devices: a whole 4x4x4 slice. The times are simulated.
128 devices in a mesh: gx: 8 (over z, x_hi), gy: 16 (over x_lo, y, core).
Axes of the slice: x: 4 (x_hi: 2, x_lo: 2; x = x_hi * 2 + x_lo), y: 4, z: 4, core: 2. Of those that a mesh axis runs over, the one named last changes fastest.
Arguments:
- source_planes: float32 [384, 384, 384], P(('gx', 'gy')), may hold values from -6 to 6
- weight_x: float32 [64, 384], replicated, may hold values from -0.3125 to 0.3125
- weight_y: float32 [96, 384], replicated, may hold values from -0.3125 to 0.3125
- weight_z: float32 [96, 384], replicated, may hold values from -0.3125 to 0.3125
- box_anchor: int32 [3], replicated, may hold values from 0 to 416, as said below
- velocity: float32 [3, 192, 512, 320], P(None, 'gx', 'gy'), may hold values from -6 to 6
- stress: float32 [6, 192, 512, 320], P(None, 'gx', 'gy'), may hold values from -6 to 6
- lame_lambda: float32 [192, 512, 320], P('gx', 'gy'), may hold values from 0.2 to 1
- lame_mu: float32 [192, 512, 320], P('gx', 'gy'), may hold values from 0.2 to 1
- buoyancy: float32 [192, 512, 320], P('gx', 'gy'), may hold values from 0.5 to 1.5
- attenuation: float32 [192, 512, 320], P('gx', 'gy'), may hold values from 0.05 to 3
Outputs:
- velocity_out: float32 [3, 192, 512, 320], P(None, 'gx', 'gy')
- stress_out: float32 [6, 192, 512, 320], P(None, 'gx', 'gy')
Inputs may be any that keep to these rules, and one draw needn't show every extreme that they name: The box of 64 x 96 x 96 cells that starts at box_anchor lies inside the thorax grid; along the dimension with the most room it ends at the grid's far side, along one of the other two it starts at cell 0.
All inputs are finite; a program needn't handle non-finite values.
Results may differ from a plain program's by a relative error of at most 0.00005.
Values sent between devices are 32-bit elements; how exact they have to be, the bound alone decides.
No kernel may reach another device: no remote copies, remote signals or barrier semaphores. Data moves between devices by JAX's collectives and lax.ppermute only.
A program may use at most 128 MiB of HBM per device.

v0:
```python
import jax
import jax.numpy as jnp
from jax import lax
from jax.sharding import PartitionSpec as P

STEPS = 2
time_step = 0.2
precise = lax.Precision.HIGHEST


def from_behind(value, axis, by):
    size = lax.axis_size(axis)
    pairs = [(i, i + by) for i in range(size) if 0 <= i + by < size]
    return lax.ppermute(value, axis, pairs)


def back_diff(values, dimension, beside):
    count = values.shape[dimension]
    return values - jnp.concatenate(
        [beside, lax.slice_in_dim(values, 0, count - 1, axis=dimension)], dimension
    )


def ahead_diff(values, dimension, beside):
    count = values.shape[dimension]
    return (
        jnp.concatenate([lax.slice_in_dim(values, 1, count, axis=dimension), beside], dimension)
        - values
    )


def one_hot(anchor, amount, box_start, extent):
    positions = anchor + lax.iota(jnp.int32, amount) - box_start
    return (positions[:, None] == lax.iota(jnp.int32, extent)[None, :]).astype(jnp.float32)


def shards(
    source_planes,
    weight_x,
    weight_y,
    weight_z,
    box_anchor,
    velocity,
    stress,
    lame_lambda,
    lame_mu,
    buoyancy,
    attenuation,
):
    rows_x = velocity.shape[1]
    rows_y = velocity.shape[2]
    cells_z = velocity.shape[3]
    box_x = weight_x.shape[0]
    box_y = weight_y.shape[0]
    box_z = weight_z.shape[0]
    reduced = jnp.einsum("abc,zc->abz", source_planes, weight_z, precision=precise)
    reduced = jnp.einsum("abz,yb->ayz", reduced, weight_y, precision=precise)
    own_planes = reduced.shape[0]
    own_start = lax.axis_index(("gx", "gy")) * own_planes
    weight_own = lax.dynamic_slice_in_dim(weight_x, own_start, own_planes, 1)
    partial_box = jnp.einsum("xa,ayz->xyz", weight_own, reduced, precision=precise)
    whole_box = lax.psum(partial_box, ("gx", "gy"))
    place_x = one_hot(lax.axis_index("gx") * rows_x, rows_x, box_anchor[0], box_x)
    box_rows = jnp.einsum("Xx,xyz->Xyz", place_x, whole_box, precision=precise)
    place_y = one_hot(lax.axis_index("gy") * rows_y, rows_y, box_anchor[1], box_y)
    place_z = one_hot(0, cells_z, box_anchor[2], box_z)
    pressure = jnp.einsum("xyz,Yy->xYz", box_rows, place_y, precision=precise)
    pressure = jnp.einsum("xYz,Zz->xYZ", pressure, place_z, precision=precise)
    decay = jnp.exp(-time_step * attenuation)
    zero_z = jnp.zeros((rows_x, rows_y, 1), jnp.float32)
    speed_x, speed_y, speed_z = (velocity[0], velocity[1], velocity[2])
    stress_xx, stress_yy, stress_zz = (stress[0], stress[1], stress[2])
    stress_xy, stress_xz, stress_yz = (stress[3], stress[4], stress[5])
    for stepping in range(STEPS):
        lower_x = from_behind(jnp.stack([stress_xx[-1], stress_xy[-1], stress_xz[-1]]), "gx", 1)
        lower_y = from_behind(
            jnp.stack([stress_xy[:, -1], stress_yy[:, -1], stress_yz[:, -1]]), "gy", 1
        )
        speed_x = speed_x + time_step * buoyancy * (
            back_diff(stress_xx, 0, lower_x[0][None])
            + back_diff(stress_xy, 1, lower_y[0][:, None])
            + back_diff(stress_xz, 2, zero_z)
        )
        speed_y = speed_y + time_step * buoyancy * (
            back_diff(stress_xy, 0, lower_x[1][None])
            + back_diff(stress_yy, 1, lower_y[1][:, None])
            + back_diff(stress_yz, 2, zero_z)
        )
        speed_z = speed_z + time_step * buoyancy * (
            back_diff(stress_xz, 0, lower_x[2][None])
            + back_diff(stress_yz, 1, lower_y[2][:, None])
            + back_diff(stress_zz, 2, zero_z)
        )
        upper_x = from_behind(jnp.stack([speed_x[0], speed_y[0], speed_z[0]]), "gx", -1)
        upper_y = from_behind(jnp.stack([speed_x[:, 0], speed_y[:, 0], speed_z[:, 0]]), "gy", -1)
        strain_xx = ahead_diff(speed_x, 0, upper_x[0][None])
        strain_yy = ahead_diff(speed_y, 1, upper_y[1][:, None])
        strain_zz = ahead_diff(speed_z, 2, zero_z)
        trace = strain_xx + strain_yy + strain_zz
        shear_xy = ahead_diff(speed_x, 1, upper_y[0][:, None]) + ahead_diff(
            speed_y, 0, upper_x[1][None]
        )
        shear_xz = ahead_diff(speed_x, 2, zero_z) + ahead_diff(speed_z, 0, upper_x[2][None])
        shear_yz = ahead_diff(speed_y, 2, zero_z) + ahead_diff(speed_z, 1, upper_y[2][:, None])
        stress_xx = decay * (
            stress_xx
            + time_step * (lame_lambda * trace + 2.0 * lame_mu * strain_xx)
            - time_step * pressure
        )
        stress_yy = decay * (
            stress_yy
            + time_step * (lame_lambda * trace + 2.0 * lame_mu * strain_yy)
            - time_step * pressure
        )
        stress_zz = decay * (
            stress_zz
            + time_step * (lame_lambda * trace + 2.0 * lame_mu * strain_zz)
            - time_step * pressure
        )
        stress_xy = decay * (stress_xy + time_step * lame_mu * shear_xy)
        stress_xz = decay * (stress_xz + time_step * lame_mu * shear_xz)
        stress_yz = decay * (stress_yz + time_step * lame_mu * shear_yz)
    velocity_out = jnp.stack([speed_x, speed_y, speed_z])
    stress_out = jnp.stack([stress_xx, stress_yy, stress_zz, stress_xy, stress_xz, stress_yz])
    return (velocity_out, stress_out)


def solution(mesh):
    in_specs = (
        P(("gx", "gy"), None, None),
        P(),
        P(),
        P(),
        P(),
        P(None, "gx", "gy", None),
        P(None, "gx", "gy", None),
        P("gx", "gy", None),
        P("gx", "gy", None),
        P("gx", "gy", None),
        P("gx", "gy", None),
    )
    out_specs = (P(None, "gx", "gy", None), P(None, "gx", "gy", None))
    return jax.shard_map(shards, mesh=mesh, in_specs=in_specs, out_specs=out_specs, check_vma=False)
```

profile of v0, /device:TPU:6, one launch (start us, length us, event | category | flops | bytes accessed | tf_op | source)
XLA Modules:
  0.0 261.1 jit_solution(14584826044277785940)
XLA Ops:
  7.2 4.8 %slice_bitcast_fusion.1 = (f32[24,32,320]{2,1,0:T(8,128)}, f32[24,32,320]{2,1,0:T(8,128)S(1)}, f32[24,32,320]{2,1,0:T(8,128)S(1)}, f32[24,32,320]{2,1,0:T(8,128)S(1)}, f32[24,32,320]{2,1,0:T(8,128)}) fusion(f32[6,24,32,320]{3,2,1,0:T(8,128)} %param.17), kind=kLoop, calls=%fused_computation.98 | loop fusion | bytes 9830400 | tf_op jit(solution)/shard_map/squeeze | solution.py:73
  12.1 1.0 copy-done.20
  13.1 0.3 copy-done.22
  13.6 1.9 collective-permute-start.1
  15.5 0.9 slice_bitcast_fusion.10
  16.4 4.7 %collective-permute-start = (f32[3,32,320]{2,1,0:T(8,128)S(1)}, f32[3,32,320]{2,1,0:T(8,128)S(1)}, u32[]{:S(2)}, u32[]{:S(2)}) collective-permute-start(f32[3,32,320]{2,1,0:T(8,128)S(1)} %pad_maximum_fusion.1), channel_id=1, source_target_pairs={{0,16},{16,32},{32,48},{48,64},{64,80},{80,96},{96,112},{1,17},{17... | collective-permute-start | bytes 368648 | tf_op jit(solution)/shard_map/ppermute | solution.py:14
  21.1 1.6 fusion.60
  22.7 1.1 convolution_bitcast_fusion.1
  23.9 3.5 %fusion.65 = f32[64,96,96]{2,0,1:T(8,128)S(1)} fusion(f32[3,96,96]{2,0,1:T(4,128)S(1)} %copy.13, f32[64,384]{1,0:T(8,128)} %param.12, s32[]{:T(128)S(6)} %select_n.3), kind=kOutput, calls=%fused_computation.147 | convolution fusion | flops 21233664 | bytes 2502660 | tf_op jit(solution)/shard_map/xa,ayz->xyz/dot_general | solution.py:61
  27.5 3.5 %copy.14 = f32[64,96,96]{2,1,0:T(8,128)} copy(f32[64,96,96]{2,0,1:T(8,128)S(1)} %fusion.65) | data formatting | bytes 4718592 | tf_op jit(solution)/shard_map/xa,ayz->xyz/dot_general | solution.py:61
  31.0 3.9 %slice_bitcast_fusion.7 = (f32[23,32,320]{2,1,0:T(8,128)}, f32[23,32,320]{2,1,0:T(8,128)}, f32[23,32,320]{2,1,0:T(8,128)}) fusion(f32[6,24,32,320]{3,2,1,0:T(8,128)} %param.17), kind=kLoop, calls=%fused_computation.105 | loop fusion | bytes 5652480 | tf_op jit(solution)/shard_map/slice | solution.py:20
  34.9 0.7 fusion.79
  35.6 0.7 iota_subtract_fusion
  36.3 0.7 add_subtract_fusion
  37.0 0.6 add_subtract_fusion.1
  37.7 1.2 slice_bitcast_fusion.31
  38.9 6.4 %fusion.5 = (f32[24,32,320]{2,1,0:T(8,128)S(1)}, f32[24,32,320]{2,1,0:T(8,128)S(1)}) fusion(f32[23,32,320]{2,1,0:T(8,128)} %get-tuple-element.17, f32[1,32,320]{2,1,0:T(8,128)S(1)} %get-tuple-element.46, f32[24,31,320]{2,1,0:T(8,128)} %bitcast.189, f32[24,1,320]{2,1,0:T(1,128)S(1)} %get-tuple-element.43, f32[24,32,319]{2,1,0:T(8,128)} %bitcast.190, ...), kind=kLoop, calls=%fused_computation.9 | loop fusion | flops 4669440 | bytes 15722496 | tf_op jit(solution)/shard_map/add | solution.py:79
  45.5 0.9 slice-done.1
  46.3 1.0 copy-done.21
  47.3 0.5 copy-done.25
  47.8 2.4 fusion.9
  50.3 1.2 slice.421
  51.4 1.4 slice.439
  52.8 1.2 slice.455
  54.1 1.2 slice.434
  55.3 1.4 slice.454
  56.7 1.2 slice.441
  57.8 0.4 slice.446
  58.4 5.1 %collective-permute-start.3 = (f32[3,24,320]{2,0,1:T(4,128)S(1)}, f32[3,24,320]{2,0,1:T(4,128)S(1)}, u32[]{:S(2)}, u32[]{:S(2)}) collective-permute-start(f32[3,24,320]{2,0,1:T(4,128)S(1)} %pad_maximum_fusion.4), channel_id=1, source_target_pairs={{1,0},{2,1},{3,2},{4,3},{5,4},{6,5},{7,6},{8,7},{9,8},{10,9},{11,1... | collective-permute-start | bytes 276488 | tf_op jit(solution)/shard_map/ppermute | solution.py:14
  63.5 4.1 %collective-permute-start.2 = (f32[3,32,320]{2,1,0:T(8,128)S(1)}, f32[3,32,320]{2,1,0:T(8,128)S(1)}, u32[]{:S(2)}, u32[]{:S(2)}) collective-permute-start(f32[3,32,320]{2,1,0:T(8,128)S(1)} %pad_maximum_fusion.3), channel_id=1, source_target_pairs={{16,0},{32,16},{48,32},{64,48},{80,64},{96,80},{112,96},{17,1},{33... | collective-permute-start | bytes 368648 | tf_op jit(solution)/shard_map/ppermute | solution.py:14
  67.8 5.4 %collective-permute-done.2 = f32[3,32,320]{2,1,0:T(8,128)S(1)} collective-permute-done((f32[3,32,320]{2,1,0:T(8,128)S(1)}, f32[3,32,320]{2,1,0:T(8,128)S(1)}, u32[]{:S(2)}, u32[]{:S(2)}) %collective-permute-start.2) | collective-permute-done | bytes 122912 | tf_op jit(solution)/shard_map/ppermute | solution.py:14
  73.2 0.9 fusion.21
  74.2 1.0 copy-done.11
  75.2 1.1 slice.467
  76.2 109.6 %all-reduce.14.cloned.1.call-done = f32[64,96,96]{2,1,0:T(8,128)} async-done(((f32[64,96,96]{2,1,0:T(8,128)}), f32[64,96,96]{2,1,0:T(8,128)}) %all-reduce.14.cloned.1.call-update) | async-done | bytes 2359312 | tf_op jit(solution)/shard_map/psum | solution.py:62
  185.9 4.9 %fusion = f32[24,96,96]{2,0,1:T(8,128)S(1)} fusion(f32[64,96,96]{2,1,0:T(8,128)} %all-reduce.14.cloned.1.call-done, s32[24]{0:T(128)S(1)} %add_subtract_fusion), kind=kOutput, calls=%fused_computation.1 | convolution fusion | flops 169870848 | bytes 3244128 | tf_op jit(solution)/shard_map/Xx,xyz->Xyz/dot_general | solution.py:64
  190.8 0.6 convolution_bitcast_fusion
  191.5 0.6 copy-done.6
  192.0 5.2 %subtract_multiply_fusion = (f32[24,32,320]{2,1,0:T(8,128)}, f32[24,32,320]{2,1,0:T(8,128)S(1)}, f32[24,32,320]{2,1,0:T(8,128)S(1)}, f32[24,32,320]{2,1,0:T(8,128)S(1)}) fusion(f32[24,32,320]{2,1,0:T(8,128)S(1)} %copy-done.2, f32[24,32,320]{2,1,0:T(8,128)S(1)} %copy-done.8, f32[24,32,319]{2,1,0:T(8,128)} %slice.439, f32[6,24,32,320]{3,2,1,0:T(8,128)} %param.17, ...), kind=kOutput, calls=%fused_computation.92 | convolution fusion | flops 289290240 | bytes 17001728 | tf_op jit(solution)/shard_map/xYz,Zz->xYZ/dot_general | solution.py:68
  197.2 0.5 copy-done.24
  197.7 2.2 subtract_multiply_fusion.1
  200.0 0.9 copy-done.16
  200.9 1.1 slice.451
  202.2 1.9 collective-permute-start.5
  204.1 3.5 %collective-permute-start.4 = (f32[3,32,320]{2,1,0:T(8,128)S(1)}, f32[3,32,320]{2,1,0:T(8,128)S(1)}, u32[]{:S(2)}, u32[]{:S(2)}) collective-permute-start(f32[3,32,320]{2,1,0:T(8,128)S(1)} %pad_maximum_fusion.5), channel_id=1, source_target_pairs={{0,16},{16,32},{32,48},{48,64},{64,80},{80,96},{96,112},{1,17},{17... | collective-permute-start | bytes 368648 | tf_op jit(solution)/shard_map/ppermute | solution.py:14
  207.6 3.1 %collective-permute-done.5 = f32[3,24,320]{2,0,1:T(4,128)S(1)} collective-permute-done((f32[3,24,320]{2,0,1:T(4,128)S(1)}, f32[3,24,320]{2,0,1:T(4,128)S(1)}, u32[]{:S(2)}, u32[]{:S(2)}) %collective-permute-start.5) | collective-permute-done | bytes 92192 | tf_op jit(solution)/shard_map/ppermute | solution.py:14
  210.8 3.1 %collective-permute-done.4 = f32[3,32,320]{2,1,0:T(8,128)S(1)} collective-permute-done((f32[3,32,320]{2,1,0:T(8,128)S(1)}, f32[3,32,320]{2,1,0:T(8,128)S(1)}, u32[]{:S(2)}, u32[]{:S(2)}) %collective-permute-start.4) | collective-permute-done | bytes 122912 | tf_op jit(solution)/shard_map/ppermute | solution.py:14
  213.9 1.1 fusion.33
  215.2 5.1 %fusion.25 = (f32[24,32,320]{2,1,0:T(8,128)S(1)}, f32[24,32,320]{2,1,0:T(8,128)S(1)}) fusion(f32[24,32,320]{2,1,0:T(8,128)S(1)} %copy-done.6, f32[24,32,320]{2,1,0:T(8,128)} %copy-done.16, f32[23,32,320]{2,1,0:T(8,128)} %slice.451, f32[1,32,320]{2,1,0:T(8,128)S(1)} %get-tuple-element.34, f32[24,32,320]{2,1,0:T(8,128)S(1)} %get-tuple-element.8, ...), kind=kLoop, calls=%fused_computation.40 | loop fusion | flops 4669440 | bytes 15722496 | tf_op jit(solution)/shard_map/add | solution.py:79
  220.5 0.4 slice.481
  220.9 1.1 slice.471
  221.9 1.1 slice.484
  223.2 0.4 slice.486
  223.7 0.4 slice.489
  224.3 4.6 %collective-permute-start.7 = (f32[3,24,320]{2,0,1:T(4,128)S(1)}, f32[3,24,320]{2,0,1:T(4,128)S(1)}, u32[]{:S(2)}, u32[]{:S(2)}) collective-permute-start(f32[3,24,320]{2,0,1:T(4,128)S(1)} %pad_maximum_fusion.8), channel_id=1, source_target_pairs={{1,0},{2,1},{3,2},{4,3},{5,4},{6,5},{7,6},{8,7},{9,8},{10,9},{11,1... | collective-permute-start | bytes 276488 | tf_op jit(solution)/shard_map/ppermute | solution.py:14
  228.9 2.1 pad_maximum_fusion
  231.0 2.6 collective-permute-start.6
  233.7 6.8 %collective-permute-done.6 = f32[3,32,320]{2,1,0:T(8,128)S(1)} collective-permute-done((f32[3,32,320]{2,1,0:T(8,128)S(1)}, f32[3,32,320]{2,1,0:T(8,128)S(1)}, u32[]{:S(2)}, u32[]{:S(2)}) %collective-permute-start.6) | collective-permute-done | bytes 122912 | tf_op jit(solution)/shard_map/ppermute | solution.py:14
  240.5 3.8 %bitcast_dynamic-update-slice_fusion.2 = (f32[6,24,32,320]{3,2,1,0:T(8,128)}, f32[24,32,320]{2,1,0:T(8,128)S(1)}) fusion(f32[24,32,320]{2,1,0:T(8,128)S(1)} %get-tuple-element.52, f32[24,32,320]{2,1,0:T(8,128)S(1)} %copy-done.17, f32[24,32,320]{2,1,0:T(8,128)S(1)} %copy-done.2, f32[24,32,320]{2,1,0:T(8,128)S(1)} %get-tuple-element.23, ...), kind=kLoop, calls=%fused_computation.85 | loop fusion | flops 3932159 | bytes 12973056
  244.3 2.0 bitcast_dynamic-update-slice_fusion.1
  246.3 2.0 bitcast_dynamic-update-slice_fusion
  248.3 2.0 fusion.43
  250.3 2.0 fusion.49
  252.3 2.0 fusion.55
  (112 shorter events, 2.3 us)
Async XLA Ops:
  7.2 13.9 %copy-start = (f32[3,384,384]{2,1,0:T(8,128)S(1)}, f32[3,384,384]{2,1,0:T(8,128)}, u32[]{:S(2)}) copy-start(f32[3,384,384]{2,1,0:T(8,128)} %param.11) | copy-start | bytes 5308420
  7.2 178.7 %all-reduce.14.cloned.1.call-start = ((), (), s32[]{:S(2)}) async-start(), calls=%async_computation | async-start | bytes 6291456 | tf_op jit(solution)/shard_map/psum | solution.py:62
  12.0 1.0 copy-start.20
  12.0 1.4 copy-start.22
  12.0 9.0 %copy-start.27 = (f32[96,384]{1,0:T(8,128)S(1)}, f32[96,384]{1,0:T(8,128)}, u32[]{:S(2)}) copy-start(f32[96,384]{1,0:T(8,128)} %param.14) | copy-start | bytes 442372
  13.6 24.1 %collective-permute-start.1 = (f32[3,24,320]{2,0,1:T(4,128)S(1)}, f32[3,24,320]{2,0,1:T(4,128)}, u32[]{:S(2)}, u32[]{:S(2)}) collective-permute-start(f32[3,24,320]{2,0,1:T(4,128)S(1)} %pad_maximum_fusion.2), channel_id=1, source_target_pairs={{0,1},{1,2},{2,3},{3,4},{4,5},{5,6},{6,7},{7,8},{8,9},{9,10},{10,1... | collective-permute-start | bytes 276488 | tf_op jit(solution)/shard_map/ppermute | solution.py:14
  16.4 22.5 %collective-permute-start = (f32[3,32,320]{2,1,0:T(8,128)S(1)}, f32[3,32,320]{2,1,0:T(8,128)S(1)}, u32[]{:S(2)}, u32[]{:S(2)}) collective-permute-start(f32[3,32,320]{2,1,0:T(8,128)S(1)} %pad_maximum_fusion.1), channel_id=1, source_target_pairs={{0,16},{16,32},{32,48},{48,64},{64,80},{80,96},{96,112},{1,17},{17... | collective-permute-start | bytes 368648 | tf_op jit(solution)/shard_map/ppermute | solution.py:14
  21.1 1.6 copy-start.28
  31.0 4.0 %copy-start.29 = (s32[3]{0:T(128)S(1)}, s32[3]{0:T(128)}, u32[]{:S(2)}) copy-start(s32[3]{0:T(128)} %param.15) | copy-start | bytes 40
  31.0 7.9 %copy-start.13 = (f32[24,32,320]{2,1,0:T(8,128)S(1)}, f32[24,32,320]{2,1,0:T(8,128)}, u32[]{:S(2)}) copy-start(f32[24,32,320]{2,1,0:T(8,128)} %param.20) | copy-start | bytes 2949124
  38.9 6.6 %slice-start = ((s8[7077888]{0:T(1024)(128)(4,1)}), s8[4194304]{0:T(1024)(128)(4,1)S(1)}, s32[]{:S(2)}) async-start(s8[7077888]{0:T(1024)(128)(4,1)} %bitcast.175), calls=%async_computation.1 | async-start | bytes 8388608
  38.9 7.5 %slice-start.1 = ((s8[7077888]{0:T(1024)(128)(4,1)}), s8[2883584]{0:T(1024)(128)(4,1)S(1)}, s32[]{:S(2)}) async-start(s8[7077888]{0:T(1024)(128)(4,1)} %bitcast.175), calls=%async_computation.2 | async-start | bytes 5767168
  38.9 8.4 %copy-start.21 = (f32[24,32,320]{2,1,0:T(8,128)S(1)}, f32[24,32,320]{2,1,0:T(8,128)}, u32[]{:S(2)}) copy-start(f32[24,32,320]{2,1,0:T(8,128)} %copy-done.20) | copy-start | bytes 2949124
  38.9 8.9 %copy-start.25 = (f32[23,32,320]{2,1,0:T(8,128)S(1)}, f32[23,32,320]{2,1,0:T(8,128)}, u32[]{:S(2)}) copy-start(f32[23,32,320]{2,1,0:T(8,128)} %get-tuple-element.18) | copy-start | bytes 2826244
  45.4 27.8 %copy-start.5 = (f32[24,32,320]{2,1,0:T(8,128)}, f32[24,32,320]{2,1,0:T(8,128)S(1)}, u32[]{:S(2)}) copy-start(f32[24,32,320]{2,1,0:T(8,128)S(1)} %get-tuple-element.10) | copy-start | bytes 2949124
  45.4 27.8 %copy-start.7 = (f32[24,32,320]{2,1,0:T(8,128)}, f32[24,32,320]{2,1,0:T(8,128)S(1)}, u32[]{:S(2)}) copy-start(f32[24,32,320]{2,1,0:T(8,128)S(1)} %get-tuple-element.11) | copy-start | bytes 2949124
  50.2 7.6 %copy-start.9 = (f32[24,32,320]{2,1,0:T(8,128)}, f32[24,32,320]{2,1,0:T(8,128)S(1)}, u32[]{:S(2)}) copy-start(f32[24,32,320]{2,1,0:T(8,128)S(1)} %fusion.9) | copy-start | bytes 2949124
  58.2 5.3 %slice-start.4 = ((f32[24,32,320]{2,1,0:T(8,128)}), f32[1,32,320]{2,1,0:T(8,128)S(1)}, s32[]{:S(2)}) async-start(f32[24,32,320]{2,1,0:T(8,128)} %copy-done.9), calls=%async_computation.5 | async-start | bytes 98304 | tf_op jit(solution)/shard_map/slice | solution.py:94
  58.2 15.0 %copy-start.2 = (f32[24,32,320]{2,1,0:T(8,128)S(1)}, f32[24,32,320]{2,1,0:T(8,128)}, u32[]{:S(2)}) copy-start(f32[24,32,320]{2,1,0:T(8,128)} %param.19) | copy-start | bytes 2949124
  58.2 15.0 %copy-start.3 = (f32[24,32,320]{2,1,0:T(8,128)S(1)}, f32[24,32,320]{2,1,0:T(8,128)}, u32[]{:S(2)}) copy-start(f32[24,32,320]{2,1,0:T(8,128)} %param.21) | copy-start | bytes 2949124
  58.4 9.3 %collective-permute-start.3 = (f32[3,24,320]{2,0,1:T(4,128)S(1)}, f32[3,24,320]{2,0,1:T(4,128)S(1)}, u32[]{:S(2)}, u32[]{:S(2)}) collective-permute-start(f32[3,24,320]{2,0,1:T(4,128)S(1)} %pad_maximum_fusion.4), channel_id=1, source_target_pairs={{1,0},{2,1},{3,2},{4,3},{5,4},{6,5},{7,6},{8,7},{9,8},{10,9},{11,1... | collective-permute-start | bytes 276488 | tf_op jit(solution)/shard_map/ppermute | solution.py:14
  63.5 9.6 %collective-permute-start.2 = (f32[3,32,320]{2,1,0:T(8,128)S(1)}, f32[3,32,320]{2,1,0:T(8,128)S(1)}, u32[]{:S(2)}, u32[]{:S(2)}) collective-permute-start(f32[3,32,320]{2,1,0:T(8,128)S(1)} %pad_maximum_fusion.3), channel_id=1, source_target_pairs={{16,0},{32,16},{48,32},{64,48},{80,64},{96,80},{112,96},{17,1},{33... | collective-permute-start | bytes 368648 | tf_op jit(solution)/shard_map/ppermute | solution.py:14
  74.2 1.0 copy-start.11
  185.9 5.6 %copy-start.8 = (f32[24,32,320]{2,1,0:T(8,128)S(1)}, f32[24,32,320]{2,1,0:T(8,128)}, u32[]{:S(2)}) copy-start(f32[24,32,320]{2,1,0:T(8,128)} %copy-done.7) | copy-start | bytes 2949124
  185.9 5.6 %copy-start.10 = (f32[24,32,320]{2,1,0:T(8,128)S(1)}, f32[24,32,320]{2,1,0:T(8,128)}, u32[]{:S(2)}) copy-start(f32[24,32,320]{2,1,0:T(8,128)} %copy-done.9) | copy-start | bytes 2949124
  185.9 5.6 %copy-start.18 = (f32[24,31,320]{2,1,0:T(8,128)S(1)}, f32[24,31,320]{2,1,0:T(8,128)}, u32[]{:S(2)}) copy-start(f32[24,31,320]{2,1,0:T(8,128)} %slice.434) | copy-start | bytes 2856964
  185.9 5.6 %copy-start.19 = (f32[23,32,320]{2,1,0:T(8,128)S(1)}, f32[23,32,320]{2,1,0:T(8,128)}, u32[]{:S(2)}) copy-start(f32[23,32,320]{2,1,0:T(8,128)} %slice.421) | copy-start | bytes 2826244
  190.8 1.3 copy-start.6
  191.4 5.8 %slice-start.2 = ((s8[7077888]{0:T(1024)(128)(4,1)}), s8[4194304]{0:T(1024)(128)(4,1)S(1)}, s32[]{:S(2)}) async-start(s8[7077888]{0:T(1024)(128)(4,1)} %bitcast.177), calls=%async_computation.3 | async-start | bytes 8388608
  192.0 5.2 %slice-start.3 = ((s8[7077888]{0:T(1024)(128)(4,1)}), s8[2883584]{0:T(1024)(128)(4,1)S(1)}, s32[]{:S(2)}) async-start(s8[7077888]{0:T(1024)(128)(4,1)} %bitcast.177), calls=%async_computation.4 | async-start | bytes 5767168
  192.0 5.2 %slice-start.5 = ((f32[24,32,320]{2,1,0:T(8,128)}), f32[23,32,320]{2,1,0:T(8,128)S(1)}, s32[]{:S(2)}) async-start(f32[24,32,320]{2,1,0:T(8,128)} %copy-done.9), calls=%async_computation.6 | async-start | bytes 2260992 | tf_op jit(solution)/shard_map/slice | solution.py:27
  192.0 5.6 %copy-start.24 = (f32[24,31,320]{2,1,0:T(8,128)S(1)}, f32[24,31,320]{2,1,0:T(8,128)}, u32[]{:S(2)}) copy-start(f32[24,31,320]{2,1,0:T(8,128)} %slice.441) | copy-start | bytes 2856964
  199.9 1.0 copy-start.16
  200.9 13.0 %copy-start.14 = (f32[24,32,320]{2,1,0:T(8,128)S(1)}, f32[24,32,320]{2,1,0:T(8,128)}, u32[]{:S(2)}) copy-start(f32[24,32,320]{2,1,0:T(8,128)} %param.20) | copy-start | bytes 2949124
  202.2 8.6 %collective-permute-start.5 = (f32[3,24,320]{2,0,1:T(4,128)S(1)}, f32[3,24,320]{2,0,1:T(4,128)S(1)}, u32[]{:S(2)}, u32[]{:S(2)}) collective-permute-start(f32[3,24,320]{2,0,1:T(4,128)S(1)} %pad_maximum_fusion.6), channel_id=1, source_target_pairs={{0,1},{1,2},{2,3},{3,4},{4,5},{5,6},{6,7},{7,8},{8,9},{9,10},{10,1... | collective-permute-start | bytes 276488 | tf_op jit(solution)/shard_map/ppermute | solution.py:14
  204.1 9.8 %collective-permute-start.4 = (f32[3,32,320]{2,1,0:T(8,128)S(1)}, f32[3,32,320]{2,1,0:T(8,128)S(1)}, u32[]{:S(2)}, u32[]{:S(2)}) collective-permute-start(f32[3,32,320]{2,1,0:T(8,128)S(1)} %pad_maximum_fusion.5), channel_id=1, source_target_pairs={{0,16},{16,32},{32,48},{48,64},{64,80},{80,96},{96,112},{1,17},{17... | collective-permute-start | bytes 368648 | tf_op jit(solution)/shard_map/ppermute | solution.py:14
  213.9 1.3 copy-start.12
  224.3 9.3 %collective-permute-start.7 = (f32[3,24,320]{2,0,1:T(4,128)S(1)}, f32[3,24,320]{2,0,1:T(4,128)S(1)}, u32[]{:S(2)}, u32[]{:S(2)}) collective-permute-start(f32[3,24,320]{2,0,1:T(4,128)S(1)} %pad_maximum_fusion.8), channel_id=1, source_target_pairs={{1,0},{2,1},{3,2},{4,3},{5,4},{6,5},{7,6},{8,7},{9,8},{10,9},{11,1... | collective-permute-start | bytes 276488 | tf_op jit(solution)/shard_map/ppermute | solution.py:14
  228.9 11.6 %copy-start.17 = (f32[24,32,320]{2,1,0:T(8,128)S(1)}, f32[24,32,320]{2,1,0:T(8,128)}, u32[]{:S(2)}) copy-start(f32[24,32,320]{2,1,0:T(8,128)} %copy-done.16) | copy-start | bytes 2949124
  228.9 11.6 %copy-start.23 = (f32[24,32,320]{2,1,0:T(8,128)S(1)}, f32[24,32,320]{2,1,0:T(8,128)}, u32[]{:S(2)}) copy-start(f32[24,32,320]{2,1,0:T(8,128)} %param.18) | copy-start | bytes 2949124
  231.0 9.4 %collective-permute-start.6 = (f32[3,32,320]{2,1,0:T(8,128)S(1)}, f32[3,32,320]{2,1,0:T(8,128)S(1)}, u32[]{:S(2)}, u32[]{:S(2)}) collective-permute-start(f32[3,32,320]{2,1,0:T(8,128)S(1)} %pad_maximum_fusion.7), channel_id=1, source_target_pairs={{16,0},{32,16},{48,32},{64,48},{80,64},{96,80},{112,96},{17,1},{33... | collective-permute-start | bytes 368648 | tf_op jit(solution)/shard_map/ppermute | solution.py:14
  244.3 2.0 copy-start.15
  246.3 2.0 copy-start.26
  250.3 2.0 copy-start.4
  252.2 2.0 copy-start.1
Sparse Core Ops, SparseCore 0:
  31.1 154.7 all-reduce.13
where the time goes:
time: 262 us; the launch traced here: 261 us
  waiting for transfers between devices  128 us (49%)
  local copies, waits for them, and re-layouts  36.5 us (14%)
  other arithmetic  36.4 us (14%)
  starting transfers between devices  28.4 us (11%)
  matrix products  16.9 us (6%)
  between operations  14.9 us (6%)
    psum x1, waiting for transfers between devices, shards(): whole_box = lax.psum(partial_box, ('gx', 'gy'))  110 us
    ppermute x8, starting transfers between devices, from_behind(): return lax.ppermute(value, axis, pairs)  28.4 us
    ppermute x8, waiting for transfers between devices, from_behind(): return lax.ppermute(value, axis, pairs)  18.4 us
    unnamed x7, other arithmetic  11.8 us
    slice x19, local copies, waits for them, and re-layouts, ahead_diff(): lax.slice_in_dim(values, 1, count, axis=dimension)  11.8 us
    add x2, other arithmetic, shards(): speed_x + time_step * buoyancy * (back_diff(stress_xx, 0, lower_x[0][None...  11.6 us
    unnamed x68, local copies, waits for them, and re-layouts  6.77 us
    slice x4, local copies, waits for them, and re-layouts, back_diff(): lax.slice_in_dim(values, 0, count - 1, axis=dimension)  6.17 us
  transfers between devices with their start and end apart: 9, of which 5 were waited for; matrix products, arithmetic and copies ran while one was open for 15% of the time, Pallas kernels for 0%

commit v1 on v0

--- a/solution.py
+++ b/solution.py
@@ -59,7 +59,9 @@
     own_start = lax.axis_index(("gx", "gy")) * own_planes
     weight_own = lax.dynamic_slice_in_dim(weight_x, own_start, own_planes, 1)
     partial_box = jnp.einsum("xa,ayz->xyz", weight_own, reduced, precision=precise)
-    whole_box = lax.psum(partial_box, ("gx", "gy"))
+    whole_box = partial_box
+    for mesh_axis in ("gy", "gx"):
+        whole_box = lax.psum(whole_box, mesh_axis)
     place_x = one_hot(lax.axis_index("gx") * rows_x, rows_x, box_anchor[0], box_x)
     box_rows = jnp.einsum("Xx,xyz->Xyz", place_x, whole_box, precision=precise)
     place_y = one_hot(lax.axis_index("gy") * rows_y, rows_y, box_anchor[1], box_y)

time: 262 us -> 376 us (1.44)
  waiting for transfers between devices: 128 us -> 239 us
    psum x1 -> x2, waiting for transfers between devices: 110 us -> 215 us  [shards(): whole_box = lax.psum(whole_box, mesh_axis)]
    ppermute x8, waiting for transfers between devices: 18.4 us -> 24 us  [from_behind(): return lax.ppermute(value, axis, pairs)]
    unnamed x68 -> x62, local copies, waits for them, and re-layouts: 6.77 us -> 7.75 us
    unnamed x7 -> x6, other arithmetic: 11.8 us -> 11.8 us
  transfers between devices with their start and end apart: 9 -> 10, of which waited for: 5 -> 7; matrix products, arithmetic and copies ran while one was open for 15% -> 10% of each run, Pallas kernels for 0% -> 0%
where the time goes in v1:
time: 376 us; the launch traced here: 374 us
  waiting for transfers between devices  239 us (64%)
  other arithmetic  38.3 us (10%)
  local copies, waits for them, and re-layouts  36.4 us (10%)
  starting transfers between devices  27.7 us (7%)
  matrix products  17.8 us (5%)
  between operations  14.8 us (4%)
    psum x2, waiting for transfers between devices, shards(): whole_box = lax.psum(whole_box, mesh_axis)  215 us
    ppermute x8, starting transfers between devices, from_behind(): return lax.ppermute(value, axis, pairs)  27.7 us
    ppermute x8, waiting for transfers between devices, from_behind(): return lax.ppermute(value, axis, pairs)  24 us
    slice x19, local copies, waits for them, and re-layouts, ahead_diff(): lax.slice_in_dim(values, 1, count, axis=dimension)  11.9 us
    unnamed x6, other arithmetic  11.8 us
    add x2, other arithmetic, shards(): speed_x + time_step * buoyancy * (back_diff(stress_xx, 0, lower_x[0][None...  11.1 us
    unnamed x62, local copies, waits for them, and re-layouts  7.75 us
  transfers between devices with their start and end apart: 10, of which 7 were waited for; matrix products, arithmetic and copies ran while one was open for 10% of the time, Pallas kernels for 0%

profile of v1, /device:TPU:6, one launch (start us, length us, event | category | flops | bytes accessed | tf_op | source)
XLA Modules:
  0.0 374.3 jit_solution(16402714472254907254)
XLA Ops:
  7.2 1.4 copy-done
  8.7 2.5 fusion.60
  11.2 1.1 convolution_bitcast_fusion.1
  12.5 3.5 fusion.65
  16.0 3.5 copy.14
  19.5 4.8 %slice_bitcast_fusion.1 = (f32[24,32,320]{2,1,0:T(8,128)}, f32[24,32,320]{2,1,0:T(8,128)S(1)}, f32[24,32,320]{2,1,0:T(8,128)S(1)}, f32[24,32,320]{2,1,0:T(8,128)S(1)}, f32[24,32,320]{2,1,0:T(8,128)}) fusion(f32[6,24,32,320]{3,2,1,0:T(8,128)} %param.17), kind=kLoop, calls=%fused_computation.98 | loop fusion | bytes 9830400 | tf_op jit(solution)/shard_map/squeeze | solution.py:75
  24.3 1.0 copy-done.22
  25.6 1.9 collective-permute-start.1
  27.5 0.9 slice_bitcast_fusion.10
  28.4 4.8 %collective-permute-start = (f32[3,32,320]{2,1,0:T(8,128)S(1)}, f32[3,32,320]{2,1,0:T(8,128)S(1)}, u32[]{:S(2)}, u32[]{:S(2)}) collective-permute-start(f32[3,32,320]{2,1,0:T(8,128)S(1)} %pad_maximum_fusion.1), channel_id=1, source_target_pairs={{0,16},{16,32},{32,48},{48,64},{64,80},{80,96},{96,112},{1,17},{17... | collective-permute-start | bytes 368648 | tf_op jit(solution)/shard_map/ppermute | solution.py:14
  33.3 0.6 fusion.79
  33.9 0.6 add_subtract_fusion
  34.5 0.6 iota_subtract_fusion
  35.1 3.9 %slice_bitcast_fusion.7 = (f32[23,32,320]{2,1,0:T(8,128)}, f32[23,32,320]{2,1,0:T(8,128)}, f32[23,32,320]{2,1,0:T(8,128)}) fusion(f32[6,24,32,320]{3,2,1,0:T(8,128)} %param.17), kind=kLoop, calls=%fused_computation.105 | loop fusion | bytes 5652480 | tf_op jit(solution)/shard_map/slice | solution.py:20
  39.0 0.6 add_subtract_fusion.1
  39.8 109.0 %all-reduce.15.cloned.1.call-done = f32[64,96,96]{2,1,0:T(8,128)} async-done(((f32[64,96,96]{2,1,0:T(8,128)}), f32[64,96,96]{2,1,0:T(8,128)}) %all-reduce.15.cloned.1.call-update) | async-done | bytes 2359312 | tf_op jit(solution)/shard_map/psum | solution.py:64
  148.8 1.2 copy-done.13
  150.0 6.0 %fusion.5 = (f32[24,32,320]{2,1,0:T(8,128)S(1)}, f32[24,32,320]{2,1,0:T(8,128)S(1)}) fusion(f32[23,32,320]{2,1,0:T(8,128)} %get-tuple-element.17, f32[1,32,320]{2,1,0:T(8,128)S(1)} %get-tuple-element.46, f32[24,31,320]{2,1,0:T(8,128)} %bitcast.187, f32[24,1,320]{2,1,0:T(1,128)S(1)} %get-tuple-element.43, f32[24,32,319]{2,1,0:T(8,128)} %bitcast.188, ...), kind=kLoop, calls=%fused_computation.9 | loop fusion | flops 4669440 | bytes 15722496 | tf_op jit(solution)/shard_map/add | solution.py:81
  156.0 1.2 slice.421
  157.2 1.5 slice.439
  158.7 1.2 slice.455
  159.9 0.5 copy-done.21
  160.8 3.7 fusion.9
  164.4 1.3 slice.434
  165.7 1.4 slice.454
  167.1 1.1 slice.441
  168.3 0.4 slice.446
  169.0 5.3 %collective-permute-start.3 = (f32[3,24,320]{2,0,1:T(4,128)S(1)}, f32[3,24,320]{2,0,1:T(4,128)S(1)}, u32[]{:S(2)}, u32[]{:S(2)}) collective-permute-start(f32[3,24,320]{2,0,1:T(4,128)S(1)} %pad_maximum_fusion.4), channel_id=1, source_target_pairs={{1,0},{2,1},{3,2},{4,3},{5,4},{6,5},{7,6},{8,7},{9,8},{10,9},{11,1... | collective-permute-start | bytes 276488 | tf_op jit(solution)/shard_map/ppermute | solution.py:14
  174.3 3.1 collective-permute-start.2
  177.4 4.2 %collective-permute-done.3 = f32[3,24,320]{2,0,1:T(4,128)S(1)} collective-permute-done((f32[3,24,320]{2,0,1:T(4,128)S(1)}, f32[3,24,320]{2,0,1:T(4,128)S(1)}, u32[]{:S(2)}, u32[]{:S(2)}) %collective-permute-start.3) | collective-permute-done | bytes 92192 | tf_op jit(solution)/shard_map/ppermute | solution.py:14
  181.7 7.5 %collective-permute-done.2 = f32[3,32,320]{2,1,0:T(8,128)S(1)} collective-permute-done((f32[3,32,320]{2,1,0:T(8,128)S(1)}, f32[3,32,320]{2,1,0:T(8,128)S(1)}, u32[]{:S(2)}, u32[]{:S(2)}) %collective-permute-start.2) | collective-permute-done | bytes 122912 | tf_op jit(solution)/shard_map/ppermute | solution.py:14
  189.2 2.2 fusion.21
  191.5 1.0 copy-done.11
  192.5 1.1 slice.467
  193.6 106.3 %all-reduce.17.cloned.1.call-done = f32[64,96,96]{2,1,0:T(8,128)} async-done(((f32[64,96,96]{2,1,0:T(8,128)}), f32[64,96,96]{2,1,0:T(8,128)}) %all-reduce.17.cloned.1.call-update) | async-done | bytes 2359312 | tf_op jit(solution)/shard_map/psum | solution.py:64
  299.9 4.9 %fusion = f32[24,96,96]{2,0,1:T(8,128)S(1)} fusion(f32[64,96,96]{2,1,0:T(8,128)} %all-reduce.17.cloned.1.call-done, s32[24]{0:T(128)S(1)} %add_subtract_fusion), kind=kOutput, calls=%fused_computation.1 | convolution fusion | flops 169870848 | bytes 3244128 | tf_op jit(solution)/shard_map/Xx,xyz->Xyz/dot_general | solution.py:66
  304.8 0.6 convolution_bitcast_fusion
  305.5 0.6 copy-done.6
  306.1 5.2 %subtract_multiply_fusion = (f32[24,32,320]{2,1,0:T(8,128)}, f32[24,32,320]{2,1,0:T(8,128)S(1)}, f32[24,32,320]{2,1,0:T(8,128)S(1)}, f32[24,32,320]{2,1,0:T(8,128)S(1)}) fusion(f32[24,32,320]{2,1,0:T(8,128)S(1)} %copy-done.2, f32[24,32,320]{2,1,0:T(8,128)S(1)} %copy-done.8, f32[24,32,319]{2,1,0:T(8,128)} %slice.439, f32[6,24,32,320]{3,2,1,0:T(8,128)} %param.17, ...), kind=kOutput, calls=%fused_computation.92 | convolution fusion | flops 289290240 | bytes 17001728 | tf_op jit(solution)/shard_map/xYz,Zz->xYZ/dot_general | solution.py:70
  311.2 0.5 copy-done.24
  311.7 2.2 subtract_multiply_fusion.1
  314.1 0.9 copy-done.16
  314.9 1.1 slice.451
  316.2 1.9 collective-permute-start.5
  318.1 4.2 %collective-permute-start.4 = (f32[3,32,320]{2,1,0:T(8,128)S(1)}, f32[3,32,320]{2,1,0:T(8,128)S(1)}, u32[]{:S(2)}, u32[]{:S(2)}) collective-permute-start(f32[3,32,320]{2,1,0:T(8,128)S(1)} %pad_maximum_fusion.5), channel_id=1, source_target_pairs={{0,16},{16,32},{32,48},{48,64},{64,80},{80,96},{96,112},{1,17},{17... | collective-permute-start | bytes 368648 | tf_op jit(solution)/shard_map/ppermute | solution.py:14
  322.4 2.4 collective-permute-done.5
  324.8 2.9 collective-permute-done.4
  327.7 1.1 fusion.33
  329.0 5.1 %fusion.25 = (f32[24,32,320]{2,1,0:T(8,128)S(1)}, f32[24,32,320]{2,1,0:T(8,128)S(1)}) fusion(f32[24,32,320]{2,1,0:T(8,128)S(1)} %copy-done.6, f32[24,32,320]{2,1,0:T(8,128)} %copy-done.16, f32[23,32,320]{2,1,0:T(8,128)} %slice.451, f32[1,32,320]{2,1,0:T(8,128)S(1)} %get-tuple-element.34, f32[24,32,320]{2,1,0:T(8,128)S(1)} %get-tuple-element.8, ...), kind=kLoop, calls=%fused_computation.40 | loop fusion | flops 4669440 | bytes 15722496 | tf_op jit(solution)/shard_map/add | solution.py:81
  334.3 0.4 slice.481
  334.7 1.1 slice.471
  335.8 1.1 slice.484
  337.0 0.4 slice.486
  337.5 0.4 slice.489
  338.1 4.0 %collective-permute-start.7 = (f32[3,24,320]{2,0,1:T(4,128)S(1)}, f32[3,24,320]{2,0,1:T(4,128)S(1)}, u32[]{:S(2)}, u32[]{:S(2)}) collective-permute-start(f32[3,24,320]{2,0,1:T(4,128)S(1)} %pad_maximum_fusion.8), channel_id=1, source_target_pairs={{1,0},{2,1},{3,2},{4,3},{5,4},{6,5},{7,6},{8,7},{9,8},{10,9},{11,1... | collective-permute-start | bytes 276488 | tf_op jit(solution)/shard_map/ppermute | solution.py:14
  342.2 2.1 pad_maximum_fusion
  344.2 2.4 collective-permute-start.6
  346.7 7.0 %collective-permute-done.6 = f32[3,32,320]{2,1,0:T(8,128)S(1)} collective-permute-done((f32[3,32,320]{2,1,0:T(8,128)S(1)}, f32[3,32,320]{2,1,0:T(8,128)S(1)}, u32[]{:S(2)}, u32[]{:S(2)}) %collective-permute-start.6) | collective-permute-done | bytes 122912 | tf_op jit(solution)/shard_map/ppermute | solution.py:14
  353.7 3.8 %bitcast_dynamic-update-slice_fusion.2 = (f32[6,24,32,320]{3,2,1,0:T(8,128)}, f32[24,32,320]{2,1,0:T(8,128)S(1)}) fusion(f32[24,32,320]{2,1,0:T(8,128)S(1)} %get-tuple-element.52, f32[24,32,320]{2,1,0:T(8,128)S(1)} %copy-done.17, f32[24,32,320]{2,1,0:T(8,128)S(1)} %copy-done.2, f32[24,32,320]{2,1,0:T(8,128)S(1)} %get-tuple-element.23, ...), kind=kLoop, calls=%fused_computation.85 | loop fusion | flops 3932159 | bytes 12973056
  357.6 2.0 bitcast_dynamic-update-slice_fusion.1
  359.5 2.0 bitcast_dynamic-update-slice_fusion
  361.5 2.0 fusion.43
  363.5 2.0 fusion.49
  365.5 2.0 fusion.55
  (107 shorter events, 2.7 us)
Async XLA Ops:
  7.2 1.5 copy-start
  7.2 141.6 %all-reduce.15.cloned.1.call-start = ((), (), s32[]{:S(2)}) async-start(), calls=%async_computation | async-start | bytes 6291456 | tf_op jit(solution)/shard_map/psum | solution.py:64
  8.6 2.5 copy-start.27
  19.5 13.8 %copy-start.28 = (s32[3]{0:T(128)S(1)}, s32[3]{0:T(128)}, u32[]{:S(2)}) copy-start(s32[3]{0:T(128)} %param.15) | copy-start | bytes 40
  19.5 280.4 %all-reduce.17.cloned.1.call-start = ((), (), s32[]{:S(2)}) async-start(), calls=%async_computation.1 | async-start | bytes 6291456 | tf_op jit(solution)/shard_map/psum | solution.py:64
  24.3 1.0 copy-start.22
  24.3 14.7 %copy-start.20 = (f32[24,32,320]{2,1,0:T(8,128)}, f32[24,32,320]{2,1,0:T(8,128)S(1)}, u32[]{:S(2)}) copy-start(f32[24,32,320]{2,1,0:T(8,128)S(1)} %get-tuple-element.14) | copy-start | bytes 2949124
  25.6 14.0 %collective-permute-start.1 = (f32[3,24,320]{2,0,1:T(4,128)S(1)}, f32[3,24,320]{2,0,1:T(4,128)S(1)}, u32[]{:S(2)}, u32[]{:S(2)}) collective-permute-start(f32[3,24,320]{2,0,1:T(4,128)S(1)} %pad_maximum_fusion.2), channel_id=1, source_target_pairs={{0,1},{1,2},{2,3},{3,4},{4,5},{5,6},{6,7},{7,8},{8,9},{9,10},{10,1... | collective-permute-start | bytes 276488 | tf_op jit(solution)/shard_map/ppermute | solution.py:14
  28.4 11.3 %collective-permute-start = (f32[3,32,320]{2,1,0:T(8,128)S(1)}, f32[3,32,320]{2,1,0:T(8,128)S(1)}, u32[]{:S(2)}, u32[]{:S(2)}) collective-permute-start(f32[3,32,320]{2,1,0:T(8,128)S(1)} %pad_maximum_fusion.1), channel_id=1, source_target_pairs={{0,16},{16,32},{32,48},{48,64},{64,80},{80,96},{96,112},{1,17},{17... | collective-permute-start | bytes 368648 | tf_op jit(solution)/shard_map/ppermute | solution.py:14
  148.7 1.3 copy-start.13
  156.0 33.2 %copy-start.5 = (f32[24,32,320]{2,1,0:T(8,128)}, f32[24,32,320]{2,1,0:T(8,128)S(1)}, u32[]{:S(2)}) copy-start(f32[24,32,320]{2,1,0:T(8,128)S(1)} %get-tuple-element.10) | copy-start | bytes 2949124
  156.0 33.2 %copy-start.7 = (f32[24,32,320]{2,1,0:T(8,128)}, f32[24,32,320]{2,1,0:T(8,128)S(1)}, u32[]{:S(2)}) copy-start(f32[24,32,320]{2,1,0:T(8,128)S(1)} %get-tuple-element.11) | copy-start | bytes 2949124
  158.7 1.7 copy-start.21
  158.7 2.0 copy-start.25
  164.4 4.4 %copy-start.9 = (f32[24,32,320]{2,1,0:T(8,128)}, f32[24,32,320]{2,1,0:T(8,128)S(1)}, u32[]{:S(2)}) copy-start(f32[24,32,320]{2,1,0:T(8,128)S(1)} %fusion.9) | copy-start | bytes 2949124
  168.6 20.6 %copy-start.3 = (f32[24,32,320]{2,1,0:T(8,128)S(1)}, f32[24,32,320]{2,1,0:T(8,128)}, u32[]{:S(2)}) copy-start(f32[24,32,320]{2,1,0:T(8,128)} %param.21) | copy-start | bytes 2949124
  168.7 20.5 %copy-start.2 = (f32[24,32,320]{2,1,0:T(8,128)S(1)}, f32[24,32,320]{2,1,0:T(8,128)}, u32[]{:S(2)}) copy-start(f32[24,32,320]{2,1,0:T(8,128)} %param.19) | copy-start | bytes 2949124
  169.0 12.6 %collective-permute-start.3 = (f32[3,24,320]{2,0,1:T(4,128)S(1)}, f32[3,24,320]{2,0,1:T(4,128)S(1)}, u32[]{:S(2)}, u32[]{:S(2)}) collective-permute-start(f32[3,24,320]{2,0,1:T(4,128)S(1)} %pad_maximum_fusion.4), channel_id=1, source_target_pairs={{1,0},{2,1},{3,2},{4,3},{5,4},{6,5},{7,6},{8,7},{9,8},{10,9},{11,1... | collective-permute-start | bytes 276488 | tf_op jit(solution)/shard_map/ppermute | solution.py:14
  174.3 14.9 %collective-permute-start.2 = (f32[3,32,320]{2,1,0:T(8,128)S(1)}, f32[3,32,320]{2,1,0:T(8,128)S(1)}, u32[]{:S(2)}, u32[]{:S(2)}) collective-permute-start(f32[3,32,320]{2,1,0:T(8,128)S(1)} %pad_maximum_fusion.3), channel_id=1, source_target_pairs={{16,0},{32,16},{48,32},{64,48},{80,64},{96,80},{112,96},{17,1},{33... | collective-permute-start | bytes 368648 | tf_op jit(solution)/shard_map/ppermute | solution.py:14
  191.4 1.1 copy-start.11
  299.9 5.6 %copy-start.8 = (f32[24,32,320]{2,1,0:T(8,128)S(1)}, f32[24,32,320]{2,1,0:T(8,128)}, u32[]{:S(2)}) copy-start(f32[24,32,320]{2,1,0:T(8,128)} %copy-done.7) | copy-start | bytes 2949124
  299.9 5.6 %copy-start.10 = (f32[24,32,320]{2,1,0:T(8,128)S(1)}, f32[24,32,320]{2,1,0:T(8,128)}, u32[]{:S(2)}) copy-start(f32[24,32,320]{2,1,0:T(8,128)} %copy-done.9) | copy-start | bytes 2949124
  299.9 5.6 %copy-start.18 = (f32[24,31,320]{2,1,0:T(8,128)S(1)}, f32[24,31,320]{2,1,0:T(8,128)}, u32[]{:S(2)}) copy-start(f32[24,31,320]{2,1,0:T(8,128)} %slice.434) | copy-start | bytes 2856964
  299.9 5.6 %copy-start.19 = (f32[23,32,320]{2,1,0:T(8,128)S(1)}, f32[23,32,320]{2,1,0:T(8,128)}, u32[]{:S(2)}) copy-start(f32[23,32,320]{2,1,0:T(8,128)} %slice.421) | copy-start | bytes 2826244
  304.8 1.3 copy-start.6
  305.4 5.8 %slice-start = ((s8[7077888]{0:T(1024)(128)(4,1)}), s8[4194304]{0:T(1024)(128)(4,1)S(1)}, s32[]{:S(2)}) async-start(s8[7077888]{0:T(1024)(128)(4,1)} %bitcast.175), calls=%async_computation.2 | async-start | bytes 8388608
  306.1 5.2 %slice-start.1 = ((s8[7077888]{0:T(1024)(128)(4,1)}), s8[2883584]{0:T(1024)(128)(4,1)S(1)}, s32[]{:S(2)}) async-start(s8[7077888]{0:T(1024)(128)(4,1)} %bitcast.175), calls=%async_computation.3 | async-start | bytes 5767168
  306.1 5.2 %slice-start.2 = ((f32[24,32,320]{2,1,0:T(8,128)}), f32[23,32,320]{2,1,0:T(8,128)S(1)}, s32[]{:S(2)}) async-start(f32[24,32,320]{2,1,0:T(8,128)} %copy-done.9), calls=%async_computation.4 | async-start | bytes 2260992 | tf_op jit(solution)/shard_map/slice | solution.py:27
  306.1 5.6 %copy-start.24 = (f32[24,31,320]{2,1,0:T(8,128)S(1)}, f32[24,31,320]{2,1,0:T(8,128)}, u32[]{:S(2)}) copy-start(f32[24,31,320]{2,1,0:T(8,128)} %slice.441) | copy-start | bytes 2856964
  313.9 1.0 copy-start.16
  314.9 12.8 %copy-start.14 = (f32[24,32,320]{2,1,0:T(8,128)S(1)}, f32[24,32,320]{2,1,0:T(8,128)}, u32[]{:S(2)}) copy-start(f32[24,32,320]{2,1,0:T(8,128)} %param.20) | copy-start | bytes 2949124
  316.2 8.6 %collective-permute-start.5 = (f32[3,24,320]{2,0,1:T(4,128)S(1)}, f32[3,24,320]{2,0,1:T(4,128)S(1)}, u32[]{:S(2)}, u32[]{:S(2)}) collective-permute-start(f32[3,24,320]{2,0,1:T(4,128)S(1)} %pad_maximum_fusion.6), channel_id=1, source_target_pairs={{0,1},{1,2},{2,3},{3,4},{4,5},{5,6},{6,7},{7,8},{8,9},{9,10},{10,1... | collective-permute-start | bytes 276488 | tf_op jit(solution)/shard_map/ppermute | solution.py:14
  318.1 9.6 %collective-permute-start.4 = (f32[3,32,320]{2,1,0:T(8,128)S(1)}, f32[3,32,320]{2,1,0:T(8,128)S(1)}, u32[]{:S(2)}, u32[]{:S(2)}) collective-permute-start(f32[3,32,320]{2,1,0:T(8,128)S(1)} %pad_maximum_fusion.5), channel_id=1, source_target_pairs={{0,16},{16,32},{32,48},{48,64},{64,80},{80,96},{96,112},{1,17},{17... | collective-permute-start | bytes 368648 | tf_op jit(solution)/shard_map/ppermute | solution.py:14
  327.7 1.3 copy-start.12
  338.1 8.5 %collective-permute-start.7 = (f32[3,24,320]{2,0,1:T(4,128)S(1)}, f32[3,24,320]{2,0,1:T(4,128)S(1)}, u32[]{:S(2)}, u32[]{:S(2)}) collective-permute-start(f32[3,24,320]{2,0,1:T(4,128)S(1)} %pad_maximum_fusion.8), channel_id=1, source_target_pairs={{1,0},{2,1},{3,2},{4,3},{5,4},{6,5},{7,6},{8,7},{9,8},{10,9},{11,1... | collective-permute-start | bytes 276488 | tf_op jit(solution)/shard_map/ppermute | solution.py:14
  342.1 11.6 %copy-start.17 = (f32[24,32,320]{2,1,0:T(8,128)S(1)}, f32[24,32,320]{2,1,0:T(8,128)}, u32[]{:S(2)}) copy-start(f32[24,32,320]{2,1,0:T(8,128)} %copy-done.16) | copy-start | bytes 2949124
  342.1 11.6 %copy-start.23 = (f32[24,32,320]{2,1,0:T(8,128)S(1)}, f32[24,32,320]{2,1,0:T(8,128)}, u32[]{:S(2)}) copy-start(f32[24,32,320]{2,1,0:T(8,128)} %param.18) | copy-start | bytes 2949124
  344.2 9.4 %collective-permute-start.6 = (f32[3,32,320]{2,1,0:T(8,128)S(1)}, f32[3,32,320]{2,1,0:T(8,128)S(1)}, u32[]{:S(2)}, u32[]{:S(2)}) collective-permute-start(f32[3,32,320]{2,1,0:T(8,128)S(1)} %pad_maximum_fusion.7), channel_id=1, source_target_pairs={{16,0},{32,16},{48,32},{64,48},{80,64},{96,80},{112,96},{17,1},{33... | collective-permute-start | bytes 368648 | tf_op jit(solution)/shard_map/ppermute | solution.py:14
  357.6 2.0 copy-start.15
  359.5 2.0 copy-start.26
  363.5 2.0 copy-start.4
  365.5 2.0 copy-start.1
Sparse Core Ops, SparseCore 0:
  19.6 129.0 all-reduce.14
  151.3 148.6 all-reduce.16
